TPU v7x, 32 devices: a whole 2x2x4 slice. The times are simulated.
32 devices in a mesh: expert: 4 (over x, core), shard: 8 (over z, y).
Axes of the slice: x: 2, y: 2, z: 4, core: 2. Of those that a mesh axis runs over, the one named last changes fastest.
Arguments:
- tokens_in: bfloat16 [1024, 4096], P(('expert', 'shard')), may hold values from -6 to 6
- out_grad: bfloat16 [1024, 2, 8192], P(('expert', 'shard')), may hold values from -6 to 6
- expert_ids: int32 [1024, 2], P(('expert', 'shard')), may hold values from 0 to 3, all different within a row; in each aligned block of 32 rows (0 to 31, 32 to 63, ...) at most 20 rows name the same one
- d_levels: int32 [4, 16], P('expert'), may hold values from 0 to 7
- f_levels: int32 [4, 32], P('expert', 'shard'), may hold values from 0 to 7
Outputs:
- ascent: bfloat16 [4, 4096, 8192], P('expert', None, 'shard')
Inputs may be any that keep to these rules, and one draw needn't show every extreme that they name: `expert_ids`: each token names two different experts; among the 64 entries of one device no expert is named more than 20 times, and 20 is reached on some device; every expert is named somewhere.
All inputs are finite; a program needn't handle non-finite values.
Results may differ from a plain program's by a relative error of at most 0.001.
Values may be sent and summed in bfloat16 or wider, within the bound.
A program may use at most 128 MiB of HBM per device.

v0:
```python
import jax
import jax.numpy as jnp
from jax import lax
from jax.sharding import PartitionSpec as P

BLK = 256


def invert_blocks(blocks):
    lower = jnp.linalg.cholesky(blocks)
    identity = jnp.eye(blocks.shape[-1], dtype=blocks.dtype)
    return jax.vmap(lambda factor: jax.scipy.linalg.cho_solve((factor, True), identity))(lower)


def damping(levels):
    return 0.05 * jnp.exp(0.4 * levels.astype(jnp.float32))


def covariance(rows, levels, row_count):
    blocks = rows.reshape(rows.shape[0], -1, BLK)
    cov = jnp.einsum("rbi,rbj->bij", blocks, blocks, preferred_element_type=jnp.float32) / row_count
    return cov + damping(levels)[:, None, None] * jnp.eye(BLK, dtype=jnp.float32)


def local(tokens_in, out_grad, expert_ids, d_levels, f_levels):
    group_count = lax.axis_size("expert")
    shard_count = lax.axis_size("shard")
    tok_rows = tokens_in.shape[0]
    width = tokens_in.shape[1]
    ff_full = out_grad.shape[2]
    ff_dev = ff_full // shard_count
    capacity = min(tok_rows, max(2, 5 * tok_rows // (2 * group_count)))
    slot_total = group_count * capacity
    flat_ids = expert_ids.reshape(-1)
    member = (flat_ids[:, None] == jnp.arange(group_count, dtype=jnp.int32)[None, :]).astype(
        jnp.int32
    )
    before = jnp.cumsum(member, axis=0) - member
    ranking = jnp.sum(before * member, axis=1)
    target = flat_ids * capacity + ranking
    dispatch = (jnp.arange(slot_total, dtype=jnp.int32)[:, None] == target[None, :]).astype(
        jnp.bfloat16
    )
    per_token = jnp.sum(
        dispatch.reshape(slot_total, tok_rows, 2).astype(jnp.float32), axis=2
    ).astype(jnp.bfloat16)
    x_send = jnp.dot(per_token, tokens_in, preferred_element_type=jnp.float32).astype(jnp.bfloat16)
    g_send = jnp.dot(
        dispatch, out_grad.reshape(2 * tok_rows, ff_full), preferred_element_type=jnp.float32
    ).astype(jnp.bfloat16)
    valid_slot = jnp.sum(dispatch.astype(jnp.float32), axis=1).astype(jnp.bfloat16)
    x_group, g_group, v_group = (
        lax.all_to_all(
            x_send.reshape(group_count, capacity, width),
            "expert",
            split_axis=0,
            concat_axis=1,
            tiled=True,
        ),
        lax.all_to_all(
            g_send.reshape(group_count, capacity, ff_full),
            "expert",
            split_axis=0,
            concat_axis=1,
            tiled=True,
        ),
        lax.all_to_all(
            valid_slot.reshape(group_count, capacity),
            "expert",
            split_axis=0,
            concat_axis=1,
            tiled=True,
        ),
    )
    rows_x, live_rows = (
        lax.all_gather(x_group, "shard", axis=1, tiled=True),
        lax.all_gather(v_group, "shard", axis=1, tiled=True),
    )
    rows_g = lax.all_to_all(g_group, "shard", split_axis=2, concat_axis=1, tiled=True)
    rows_x = rows_x.reshape(-1, width)
    rows_g = rows_g.reshape(-1, ff_dev)
    row_count = jnp.sum(live_rows.astype(jnp.float32))
    gradient = lax.dot_general(
        rows_x, rows_g, (((0,), (0,)), ((), ())), preferred_element_type=jnp.float32
    )
    inv_f = invert_blocks(covariance(rows_g, f_levels[0], row_count))
    grad_blocks = gradient.reshape(width // BLK, BLK, ff_dev)
    highest = lax.Precision.HIGHEST
    own_blocks = width // BLK // shard_count
    first_block = lax.axis_index("shard") * own_blocks
    own_rows = lax.dynamic_slice_in_dim(rows_x, first_block * BLK, own_blocks * BLK, 1)
    own_levels = lax.dynamic_slice_in_dim(d_levels[0], first_block, own_blocks, 0)
    inv_a = invert_blocks(covariance(own_rows, own_levels, row_count))
    left_done = jnp.einsum(
        "bij,bjf->bif",
        lax.all_gather(inv_a, "shard", axis=0, tiled=True),
        grad_blocks,
        precision=highest,
    )
    precond = jnp.einsum(
        "dcj,cjk->dck", left_done.reshape(width, ff_dev // BLK, BLK), inv_f, precision=highest
    ).reshape(width, ff_dev)
    norm_total = lax.psum(jnp.sum(precond * precond), ("expert", "shard"))
    ascent_scale = lax.rsqrt(norm_total / (group_count * width * ff_full) + 1e-06)
    return (precond * ascent_scale).astype(jnp.bfloat16)[None]


def solution(mesh):
    return jax.shard_map(
        local,
        mesh=mesh,
        in_specs=(
            P(("expert", "shard"), None),
            P(("expert", "shard"), None, None),
            P(("expert", "shard"), None),
            P("expert", None),
            P("expert", "shard"),
        ),
        out_specs=P("expert", None, "shard"),
        check_vma=False,
    )
```

profile of v0, /device:TPU:0, one launch (start us, length us, event | category | flops | bytes accessed | tf_op | source)
XLA Modules:
  0.0 676.1 jit_solution(11534804795812444572)
XLA Ops:
  9.3 15.7 %all_to_all.56 = bf16[4,20,4096]{2,1,0:T(8,128)(2,1)S(1)} all-to-all(bf16[4,20,4096]{2,1,0:T(8,128)(2,1)S(1)} %reshape.180), channel_id=1, replica_groups=mesh['expert'=4,'shard'=8] {'expert'}, dimensions={0} | all-to-all | bytes 1310720 | tf_op jit(solution)/shard_map/all_to_all | solution.py:53
  41.6 22.1 %all-reduce.2 = bf16[640]{0:T(1024)(128)(2,1)S(1)} all-reduce(bf16[640]{0:T(1024)(128)(2,1)S(1)} %dynamic-update-slice.22), channel_id=1, replica_groups=mesh['expert'=4,'shard'=8] {'shard'}, use_global_device_ids=true, to_apply=%add.2 | all-reduce | flops 640 | bytes 2560
  64.8 6.8 %copy.134 = bf16[1,80,8192]{1,0,2:T(2,128)(2,1)} copy(bf16[1,80,8192]{2,1,0:T(8,128)(2,1)S(1)} %all_to_all.42) | data formatting | bytes 2621440 | tf_op jit(solution)/shard_map/all_to_all | solution.py:60
  72.1 45.2 %reduce.30 = bf16[8192,80]{1,0:T(8,128)(2,1)S(1)} reduce(bf16[8192,1,80]{2,1,0:T(2,128)(2,1)} %bitcast.114, bf16[]{:T(256)} %broadcast.357), dimensions={1}, to_apply=%bitcast.71.reduce_sub_computation | reduce | bytes 2621442
  129.2 23.5 %custom-call.44 = f32[2,128,128]{2,1,0:T(8,128)S(1)} custom-call(f32[2,128,128]{2,1,0:T(8,128)S(1)} %cholesky.241), custom_call_target="Cholesky" | custom-call | tf_op jit(solution)/shard_map/jit(cholesky)/cholesky | solution.py:10
  153.4 19.7 %custom-call.45 = f32[2,1,128,128]{2,3,1,0:T(8,128)S(1)} custom-call(f32[2,1,128,128]{3,2,1,0:T(8,128)S(1)} %select_bitcast_fusion.1), custom_call_target="InvertDiagBlocksLowerTriangular" | custom-call | tf_op jit(solution)/shard_map/jit(cholesky)/cholesky | solution.py:10
  173.8 23.5 %custom-call.46 = f32[2,128,128]{2,1,0:T(8,128)S(1)} custom-call(f32[2,128,128]{2,1,0:T(8,128)S(1)} %convolution_subtract_fusion.5), custom_call_target="Cholesky" | custom-call | tf_op jit(solution)/shard_map/jit(cholesky)/cholesky | solution.py:10
  199.2 5.3 while.3
  204.5 40.3 %custom-call.47 = f32[2,2,128,128]{2,3,1,0:T(8,128)S(1)} custom-call(f32[2,2,128,128]{3,2,1,0:T(8,128)} %bitcast.125), custom_call_target="InvertDiagBlocksLowerTriangular" | custom-call | tf_op jit(solution)/shard_map/vmap(jit(_cho_solve))/triangular_solve | solution.py:12
  249.1 5.7 reshape.237
  254.8 8.3 %copy.135 = bf16[1,80,8192]{2,1,0:T(8,128)(2,1)S(1)} copy(bf16[1,80,8192]{1,0,2:T(2,128)(2,1)} %bitcast.115) | data formatting | bytes 2621440 | tf_op jit(solution)/shard_map/all_to_all | solution.py:79
  273.5 47.3 %custom-call.40 = f32[4,128,128]{2,1,0:T(8,128)S(1)} custom-call(f32[4,128,128]{2,1,0:T(8,128)S(1)} %cholesky.238), custom_call_target="Cholesky" | custom-call | tf_op jit(solution)/shard_map/jit(cholesky)/cholesky | solution.py:10
  321.0 39.9 %custom-call.41 = f32[4,1,128,128]{2,3,1,0:T(8,128)} custom-call(f32[4,1,128,128]{3,2,1,0:T(8,128)S(1)} %select_bitcast_fusion), custom_call_target="InvertDiagBlocksLowerTriangular" | custom-call | tf_op jit(solution)/shard_map/jit(cholesky)/cholesky | solution.py:10
  364.7 47.7 %custom-call.42 = f32[4,128,128]{2,1,0:T(8,128)S(1)} custom-call(f32[4,128,128]{2,1,0:T(8,128)} %convolution_subtract_fusion.4), custom_call_target="Cholesky" | custom-call | tf_op jit(solution)/shard_map/jit(cholesky)/cholesky | solution.py:10
  414.9 5.3 while.2
  420.2 79.6 %custom-call.43 = f32[4,2,128,128]{2,3,1,0:T(8,128)S(1)} custom-call(f32[4,2,128,128]{3,2,1,0:T(8,128)} %bitcast.124), custom_call_target="InvertDiagBlocksLowerTriangular" | custom-call | tf_op jit(solution)/shard_map/vmap(jit(_cho_solve))/triangular_solve | solution.py:12
  505.4 7.8 %copy.157 = bf16[4096,640]{1,0:T(8,128)(2,1)} copy(bf16[4096,640]{0,1:T(8,128)(2,1)} %bitcast.116) | data formatting | bytes 10485760 | tf_op jit(solution)/shard_map/dot_general | solution.py:83
  513.3 12.7 %fusion.41 = f32[16,256,1024]{2,1,0:T(8,128)} fusion(bf16[16,256,640]{2,1,0:T(8,128)(2,1)} %bitcast.117, bf16[640,1024,1]{1,0,2:T(8,128)(2,1)S(1)} %bitcast.118), kind=kOutput, calls=%fused_computation.98 | convolution fusion | flops 5368709120 | bytes 23330816 | tf_op jit(solution)/shard_map/dot_general | solution.py:83
  525.9 22.9 %fusion.42 = f32[16,256,1024]{2,1,0:T(8,128)} fusion(f32[16,256,256]{2,1,0:T(8,128)} %all-gather.5.cloned.1.call-done, f32[16,256,1024]{2,1,0:T(8,128)} %fusion.41), kind=kOutput, calls=%fused_computation.99 | convolution fusion | flops 12884901888 | bytes 37748736 | tf_op jit(solution)/shard_map/bij,bjf->bif/dot_general | solution.py:94
  548.8 20.4 %reshape.184 = f32[4096,4,256]{2,1,0:T(4,128)} reshape(f32[16,256,1024]{2,1,0:T(8,128)} %fusion.42) | data formatting | bytes 33554432 | tf_op jit(solution)/shard_map/reshape | solution.py:101
  569.2 36.8 %multiply_reduce_fusion = (f32[]{:T(128)}, f32[4,256,4096]{2,1,0:T(8,128)}) fusion(f32[4096,4,256]{2,1,0:T(4,128)} %reshape.184, f32[4,128,256]{2,1,0:T(8,128)S(1)} %fusion.14, f32[4,128,256]{2,1,0:T(8,128)S(1)} %fusion.13), kind=kOutput, calls=%fused_computation.7 | convolution fusion | flops 12893552640 | bytes 34603012 | tf_op jit(solution)/shard_map/dcj,cjk->dck/dot_general | solution.py:100
  606.0 41.1 %psum.7 = f32[]{:T(128)} all-reduce(f32[]{:T(128)} %get-tuple-element.53), channel_id=1, replica_groups=mesh['expert'=4,'shard'=8] {'expert','shard'}, use_global_device_ids=true, to_apply=%region_14.15 | all-reduce | flops 1 | bytes 8 | tf_op jit(solution)/shard_map/psum | solution.py:103
  647.8 9.1 %multiply_convert_fusion = bf16[4,256,4096]{2,1,0:T(8,128)(2,1)} fusion(f32[4,256,4096]{2,1,0:T(8,128)} %get-tuple-element.54, f32[]{:T(128)S(6)} %rsqrt.3), kind=kLoop, calls=%fused_computation.6 | loop fusion | flops 8388608 | bytes 25165828 | tf_op jit(solution)/shard_map/convert_element_type | solution.py:105
  656.9 12.0 %copy.161 = bf16[1,4096,1024]{2,1,0:T(8,128)(2,1)} copy(bf16[1,4096,1024]{1,2,0:T(8,128)(2,1)} %bitcast.113) | data formatting | bytes 16777216 | tf_op jit(solution)/shard_map/convert_element_type | solution.py:105
  (129 shorter events, 72.4 us)
Async XLA Ops:
  6.5 2.2 copy-start
  6.5 119.2 %all-gather.3.cloned.1.call-start = ((), (), s32[]{:S(2)}) async-start(), calls=%async_computation.4 | async-start | bytes 5898240 | tf_op jit(solution)/shard_map/all_gather | solution.py:76
  25.9 7.4 %copy-start.10 = (u32[32]{0:T(128)S(1)}, u32[32]{0:T(128)}, u32[]{:S(2)}) copy-start(u32[32]{0:T(128)} %constant.263) | copy-start | bytes 388
  26.8 7.9 %all-to-all-start.2 = ((bf16[4,1,20]{2,1,0:T(2,128)(2,1)}), bf16[4,1,20]{2,1,0:T(2,128)(2,1)S(1)}, u32[]{:S(2)}, u32[]{:S(2)}) async-start(bf16[4,1,20]{2,1,0:T(2,128)(2,1)} %all_to_all.51), calls=%async_computation.2 | async-start | bytes 4096 | tf_op jit(solution)/shard_map/all_to_all | solution.py:67
  31.4 7.3 %copy-start.8 = (s32[1,16]{1,0:T(1,128)S(1)}, s32[1,16]{1,0:T(1,128)}, u32[]{:S(2)}) copy-start(s32[1,16]{1,0:T(1,128)} %param.8) | copy-start | bytes 196
  34.7 29.8 %all-to-all-start = ((bf16[4,20,8192]{2,1,0:T(8,128)(2,1)}), bf16[4,20,8192]{2,1,0:T(8,128)(2,1)S(1)}, u32[]{:S(2)}, u32[]{:S(2)}) async-start(bf16[4,20,8192]{2,1,0:T(8,128)(2,1)} %reshape.179), calls=%async_computation | async-start | bytes 3145728 | tf_op jit(solution)/shard_map/all_to_all | solution.py:60
  121.9 127.1 %all-to-all-start.1 = ((bf16[8,2,40960]{2,1,0:T(2,128)(2,1)}), bf16[8,2,40960]{2,1,0:T(2,128)(2,1)S(1)}, u32[]{:S(2)}, u32[]{:S(2)}) async-start(bf16[8,2,40960]{2,1,0:T(2,128)(2,1)} %reshape.236), calls=%async_computation.1 | async-start | bytes 2621440 | tf_op jit(solution)/shard_map/all_to_all | solution.py:79
  125.5 400.4 %all-gather.5.cloned.1.call-start = ((), (), s32[]{:S(2)}) async-start(), calls=%async_computation.5 | async-start | bytes 4718592 | tf_op jit(solution)/shard_map/all_gather | solution.py:96
  197.6 51.5 %copy-start.9 = (s32[1,4]{1,0:T(1,128)S(1)}, s32[1,4]{1,0:T(1,128)}, u32[]{:S(2)}) copy-start(s32[1,4]{1,0:T(1,128)} %param.9) | copy-start | bytes 52
  269.7 51.2 %copy-start.7 = (pred[128,128]{1,0:T(8,128)(4,1)S(1)}, pred[128,128]{1,0:T(8,128)(4,1)}, u32[]{:S(2)}) copy-start(pred[128,128]{1,0:T(8,128)(4,1)} %iota_compare_fusion.3) | copy-start | bytes 49156
  271.0 142.4 %copy-start.6 = (pred[256,256]{1,0:T(8,128)(4,1)S(1)}, pred[256,256]{1,0:T(8,128)(4,1)}, u32[]{:S(2)}) copy-start(pred[256,256]{1,0:T(8,128)(4,1)} %iota_compare_fusion.2) | copy-start | bytes 196612
  272.5 1.0 copy-start.3
  360.9 139.5 %copy-start.5 = (f32[128,256]{1,0:T(8,128)S(1)}, f32[128,256]{1,0:T(8,128)}, u32[]{:S(2)}) copy-start(f32[128,256]{1,0:T(8,128)} %get-tuple-element.46) | copy-start | bytes 393220
  412.5 1.0 copy-start.2
  499.8 1.2 copy-start.4
  656.9 12.0 %copy-start.1 = (bf16[32,4096]{1,0:T(8,128)(2,1)S(1)}, bf16[32,4096]{1,0:T(8,128)(2,1)}, u32[]{:S(2)}) copy-start(bf16[32,4096]{1,0:T(8,128)(2,1)} %param.5) | copy-start | bytes 786436
Sparse Core Ops, SparseCore 0:
  26.1 86.4 all-gather.2
  249.1 74.5 all-gather.4
where the time goes:
time: 685 us; the launch traced here: 676 us
  other arithmetic  387 us (56%)
  local copies, waits for them, and re-layouts  93.3 us (14%)
  matrix products  90.7 us (13%)
  blocking collectives  79 us (12%)
  between operations  15.7 us (2%)
  starting transfers between devices  10.5 us (2%)
    another operation x18, other arithmetic, invert_blocks(): lower = jnp.linalg.cholesky(blocks)  203 us
    another operation x7, other arithmetic, invert_blocks(): jax.scipy.linalg.cho_solve((factor, True), identity)  124 us
    unnamed x3, other arithmetic  45.2 us
    psum x1, blocking collectives, local(): norm_total = lax.psum(jnp.sum(precond * precond), ('expert', 'shard'))  41.1 us
    dot_general x1, matrix products, local(): jnp.einsum('dcj,cjk->dck', left_done.reshape(width, ff_dev // BLK, BLK),...  36.8 us
    dot_general x1, matrix products, local(): jnp.einsum('bij,bjf->bif', lax.all_gather(inv_a, 'shard', axis=0, tiled=T...  22.9 us
    unnamed x1, blocking collectives  22.1 us
    reshape x1, local copies, waits for them, and re-layouts, local(): left_done.reshape(width, ff_dev // BLK, BLK)  20.4 us
  transfers between devices with their start and end apart: 5, of which 0 were waited for; matrix products, arithmetic and copies ran while one was open for 69% of the time, Pallas kernels for 0%

commit v1 on v0

--- a/solution.py
+++ b/solution.py
@@ -50,12 +50,20 @@
     ).astype(jnp.bfloat16)
     valid_slot = jnp.sum(dispatch.astype(jnp.float32), axis=1).astype(jnp.bfloat16)
     x_group, g_group, v_group = (
-        lax.all_to_all(
-            x_send.reshape(group_count, capacity, width),
-            "expert",
-            split_axis=0,
-            concat_axis=1,
-            tiled=True,
+        jnp.concatenate(
+            lax.all_to_all(
+                jnp.stack(
+                    jnp.split(
+                        x_send.reshape(group_count, capacity, width),
+                        lax.axis_size("expert"),
+                        axis=0,
+                    )
+                ),
+                "expert",
+                0,
+                0,
+            ),
+            axis=1,
         ),
         lax.all_to_all(
             g_send.reshape(group_count, capacity, ff_full),

time: 685 us -> 686 us (level)
  no operation moved by 1% of the time
where the time goes in v1:
time: 686 us; the launch traced here: 676 us
  other arithmetic  387 us (56%)
  local copies, waits for them, and re-layouts  93.3 us (14%)
  matrix products  90.7 us (13%)
  blocking collectives  79 us (12%)
  between operations  15.7 us (2%)
  starting transfers between devices  10.5 us (2%)
    another operation x18, other arithmetic, invert_blocks(): lower = jnp.linalg.cholesky(blocks)  203 us
    another operation x7, other arithmetic, invert_blocks(): jax.scipy.linalg.cho_solve((factor, True), identity)  124 us
    unnamed x3, other arithmetic  45.2 us
    psum x1, blocking collectives, local(): norm_total = lax.psum(jnp.sum(precond * precond), ('expert', 'shard'))  41.2 us
    dot_general x1, matrix products, local(): jnp.einsum('dcj,cjk->dck', left_done.reshape(width, ff_dev // BLK, BLK),...  36.8 us
    dot_general x1, matrix products, local(): jnp.einsum('bij,bjf->bif', lax.all_gather(inv_a, 'shard', axis=0, tiled=T...  22.9 us
    unnamed x1, blocking collectives  22.1 us
    reshape x1, local copies, waits for them, and re-layouts, local(): left_done.reshape(width, ff_dev // BLK, BLK)  20.4 us
  transfers between devices with their start and end apart: 5, of which 0 were waited for; matrix products, arithmetic and copies ran while one was open for 69% of the time, Pallas kernels for 0%

profile of v1, /device:TPU:0, one launch (start us, length us, event | category | flops | bytes accessed | tf_op | source)
XLA Modules:
  0.0 676.3 jit_solution(18162337235696644007)
XLA Ops:
  9.4 15.7 %all_to_all.49 = bf16[4,1,20,4096]{3,2,1,0:T(8,128)(2,1)S(1)} all-to-all(bf16[4,1,20,4096]{3,2,1,0:T(8,128)(2,1)S(1)} %pad_maximum_fusion), channel_id=1, replica_groups=mesh['expert'=4,'shard'=8] {'expert'}, dimensions={0} | all-to-all | bytes 1310720 | tf_op jit(solution)/shard_map/all_to_all | solution.py:54
  41.7 22.1 %all-reduce.2 = bf16[640]{0:T(1024)(128)(2,1)S(1)} all-reduce(bf16[640]{0:T(1024)(128)(2,1)S(1)} %dynamic-update-slice.22), channel_id=1, replica_groups=mesh['expert'=4,'shard'=8] {'shard'}, use_global_device_ids=true, to_apply=%add.2 | all-reduce | flops 640 | bytes 2560
  64.9 6.8 %copy.134 = bf16[1,80,8192]{1,0,2:T(2,128)(2,1)} copy(bf16[1,80,8192]{2,1,0:T(8,128)(2,1)S(1)} %all_to_all.36) | data formatting | bytes 2621440 | tf_op jit(solution)/shard_map/all_to_all | solution.py:68
  72.2 45.2 %reduce.30 = bf16[8192,80]{1,0:T(8,128)(2,1)S(1)} reduce(bf16[8192,1,80]{2,1,0:T(2,128)(2,1)} %bitcast.122, bf16[]{:T(256)} %broadcast.357), dimensions={1}, to_apply=%bitcast.79.reduce_sub_computation | reduce | bytes 2621442
  129.3 23.5 %custom-call.44 = f32[2,128,128]{2,1,0:T(8,128)S(1)} custom-call(f32[2,128,128]{2,1,0:T(8,128)S(1)} %cholesky.241), custom_call_target="Cholesky" | custom-call | tf_op jit(solution)/shard_map/jit(cholesky)/cholesky | solution.py:10
  153.5 19.7 %custom-call.45 = f32[2,1,128,128]{2,3,1,0:T(8,128)S(1)} custom-call(f32[2,1,128,128]{3,2,1,0:T(8,128)S(1)} %select_bitcast_fusion.1), custom_call_target="InvertDiagBlocksLowerTriangular" | custom-call | tf_op jit(solution)/shard_map/jit(cholesky)/cholesky | solution.py:10
  173.9 23.5 %custom-call.46 = f32[2,128,128]{2,1,0:T(8,128)S(1)} custom-call(f32[2,128,128]{2,1,0:T(8,128)S(1)} %convolution_subtract_fusion.5), custom_call_target="Cholesky" | custom-call | tf_op jit(solution)/shard_map/jit(cholesky)/cholesky | solution.py:10
  199.3 5.3 while.3
  204.6 40.3 %custom-call.47 = f32[2,2,128,128]{2,3,1,0:T(8,128)S(1)} custom-call(f32[2,2,128,128]{3,2,1,0:T(8,128)} %bitcast.133), custom_call_target="InvertDiagBlocksLowerTriangular" | custom-call | tf_op jit(solution)/shard_map/vmap(jit(_cho_solve))/triangular_solve | solution.py:12
  249.1 5.7 reshape.243
  254.9 8.3 %copy.135 = bf16[1,80,8192]{2,1,0:T(8,128)(2,1)S(1)} copy(bf16[1,80,8192]{1,0,2:T(2,128)(2,1)} %bitcast.123) | data formatting | bytes 2621440 | tf_op jit(solution)/shard_map/all_to_all | solution.py:87
  273.6 47.3 %custom-call.40 = f32[4,128,128]{2,1,0:T(8,128)S(1)} custom-call(f32[4,128,128]{2,1,0:T(8,128)S(1)} %cholesky.238), custom_call_target="Cholesky" | custom-call | tf_op jit(solution)/shard_map/jit(cholesky)/cholesky | solution.py:10
  321.1 39.9 %custom-call.41 = f32[4,1,128,128]{2,3,1,0:T(8,128)} custom-call(f32[4,1,128,128]{3,2,1,0:T(8,128)S(1)} %select_bitcast_fusion), custom_call_target="InvertDiagBlocksLowerTriangular" | custom-call | tf_op jit(solution)/shard_map/jit(cholesky)/cholesky | solution.py:10
  364.8 47.7 %custom-call.42 = f32[4,128,128]{2,1,0:T(8,128)S(1)} custom-call(f32[4,128,128]{2,1,0:T(8,128)} %convolution_subtract_fusion.4), custom_call_target="Cholesky" | custom-call | tf_op jit(solution)/shard_map/jit(cholesky)/cholesky | solution.py:10
  414.9 5.3 while.2
  420.3 79.6 %custom-call.43 = f32[4,2,128,128]{2,3,1,0:T(8,128)S(1)} custom-call(f32[4,2,128,128]{3,2,1,0:T(8,128)} %bitcast.132), custom_call_target="InvertDiagBlocksLowerTriangular" | custom-call | tf_op jit(solution)/shard_map/vmap(jit(_cho_solve))/triangular_solve | solution.py:12
  505.5 7.8 %copy.157 = bf16[4096,640]{1,0:T(8,128)(2,1)} copy(bf16[4096,640]{0,1:T(8,128)(2,1)} %bitcast.124) | data formatting | bytes 10485760 | tf_op jit(solution)/shard_map/dot_general | solution.py:91
  513.3 12.7 %fusion.41 = f32[16,256,1024]{2,1,0:T(8,128)} fusion(bf16[16,256,640]{2,1,0:T(8,128)(2,1)} %bitcast.125, bf16[640,1024,1]{1,0,2:T(8,128)(2,1)S(1)} %bitcast.126), kind=kOutput, calls=%fused_computation.103 | convolution fusion | flops 5368709120 | bytes 23330816 | tf_op jit(solution)/shard_map/dot_general | solution.py:91
  526.0 22.9 %fusion.42 = f32[16,256,1024]{2,1,0:T(8,128)} fusion(f32[16,256,256]{2,1,0:T(8,128)} %all-gather.5.cloned.1.call-done, f32[16,256,1024]{2,1,0:T(8,128)} %fusion.41), kind=kOutput, calls=%fused_computation.104 | convolution fusion | flops 12884901888 | bytes 37748736 | tf_op jit(solution)/shard_map/bij,bjf->bif/dot_general | solution.py:102
  548.9 20.4 %reshape.190 = f32[4096,4,256]{2,1,0:T(4,128)} reshape(f32[16,256,1024]{2,1,0:T(8,128)} %fusion.42) | data formatting | bytes 33554432 | tf_op jit(solution)/shard_map/reshape | solution.py:109
  569.3 36.8 %multiply_reduce_fusion = (f32[]{:T(128)}, f32[4,256,4096]{2,1,0:T(8,128)}) fusion(f32[4096,4,256]{2,1,0:T(4,128)} %reshape.190, f32[4,128,256]{2,1,0:T(8,128)S(1)} %fusion.14, f32[4,128,256]{2,1,0:T(8,128)S(1)} %fusion.13), kind=kOutput, calls=%fused_computation.7 | convolution fusion | flops 12893552640 | bytes 34603012 | tf_op jit(solution)/shard_map/dcj,cjk->dck/dot_general | solution.py:108
  606.1 41.2 %psum.7 = f32[]{:T(128)} all-reduce(f32[]{:T(128)} %get-tuple-element.57), channel_id=1, replica_groups=mesh['expert'=4,'shard'=8] {'expert','shard'}, use_global_device_ids=true, to_apply=%region_14.15 | all-reduce | flops 1 | bytes 8 | tf_op jit(solution)/shard_map/psum | solution.py:111
  647.9 9.1 %multiply_convert_fusion = bf16[4,256,4096]{2,1,0:T(8,128)(2,1)} fusion(f32[4,256,4096]{2,1,0:T(8,128)} %get-tuple-element.58, f32[]{:T(128)S(6)} %rsqrt.3), kind=kLoop, calls=%fused_computation.6 | loop fusion | flops 8388608 | bytes 25165828 | tf_op jit(solution)/shard_map/convert_element_type | solution.py:113
  657.1 12.0 %copy.161 = bf16[1,4096,1024]{2,1,0:T(8,128)(2,1)} copy(bf16[1,4096,1024]{1,2,0:T(8,128)(2,1)} %bitcast.121) | data formatting | bytes 16777216 | tf_op jit(solution)/shard_map/convert_element_type | solution.py:113
  (130 shorter events, 72.5 us)
Async XLA Ops:
  6.5 2.2 copy-start
  6.5 119.3 %all-gather.3.cloned.1.call-start = ((), (), s32[]{:S(2)}) async-start(), calls=%async_computation.4 | async-start | bytes 5898240 | tf_op jit(solution)/shard_map/all_gather | solution.py:84
  26.0 7.4 %copy-start.10 = (u32[32]{0:T(128)S(1)}, u32[32]{0:T(128)}, u32[]{:S(2)}) copy-start(u32[32]{0:T(128)} %constant.263) | copy-start | bytes 388
  26.9 7.9 %all-to-all-start.2 = ((bf16[4,1,20]{2,1,0:T(2,128)(2,1)}), bf16[4,1,20]{2,1,0:T(2,128)(2,1)S(1)}, u32[]{:S(2)}, u32[]{:S(2)}) async-start(bf16[4,1,20]{2,1,0:T(2,128)(2,1)} %all_to_all.44), calls=%async_computation.2 | async-start | bytes 4096 | tf_op jit(solution)/shard_map/all_to_all | solution.py:75
  31.5 7.3 %copy-start.8 = (s32[1,16]{1,0:T(1,128)S(1)}, s32[1,16]{1,0:T(1,128)}, u32[]{:S(2)}) copy-start(s32[1,16]{1,0:T(1,128)} %param.8) | copy-start | bytes 196
  34.8 29.8 %all-to-all-start = ((bf16[4,20,8192]{2,1,0:T(8,128)(2,1)}), bf16[4,20,8192]{2,1,0:T(8,128)(2,1)S(1)}, u32[]{:S(2)}, u32[]{:S(2)}) async-start(bf16[4,20,8192]{2,1,0:T(8,128)(2,1)} %reshape.185), calls=%async_computation | async-start | bytes 3145728 | tf_op jit(solution)/shard_map/all_to_all | solution.py:68
  122.0 127.1 %all-to-all-start.1 = ((bf16[8,2,40960]{2,1,0:T(2,128)(2,1)}), bf16[8,2,40960]{2,1,0:T(2,128)(2,1)S(1)}, u32[]{:S(2)}, u32[]{:S(2)}) async-start(bf16[8,2,40960]{2,1,0:T(2,128)(2,1)} %reshape.242), calls=%async_computation.1 | async-start | bytes 2621440 | tf_op jit(solution)/shard_map/all_to_all | solution.py:87
  125.6 400.4 %all-gather.5.cloned.1.call-start = ((), (), s32[]{:S(2)}) async-start(), calls=%async_computation.5 | async-start | bytes 4718592 | tf_op jit(solution)/shard_map/all_gather | solution.py:104
  197.6 51.5 %copy-start.9 = (s32[1,4]{1,0:T(1,128)S(1)}, s32[1,4]{1,0:T(1,128)}, u32[]{:S(2)}) copy-start(s32[1,4]{1,0:T(1,128)} %param.9) | copy-start | bytes 52
  269.8 51.2 %copy-start.7 = (pred[128,128]{1,0:T(8,128)(4,1)S(1)}, pred[128,128]{1,0:T(8,128)(4,1)}, u32[]{:S(2)}) copy-start(pred[128,128]{1,0:T(8,128)(4,1)} %iota_compare_fusion.3) | copy-start | bytes 49156
  271.1 142.4 %copy-start.6 = (pred[256,256]{1,0:T(8,128)(4,1)S(1)}, pred[256,256]{1,0:T(8,128)(4,1)}, u32[]{:S(2)}) copy-start(pred[256,256]{1,0:T(8,128)(4,1)} %iota_compare_fusion.2) | copy-start | bytes 196612
  272.6 1.0 copy-start.3
  361.0 139.5 %copy-start.5 = (f32[128,256]{1,0:T(8,128)S(1)}, f32[128,256]{1,0:T(8,128)}, u32[]{:S(2)}) copy-start(f32[128,256]{1,0:T(8,128)} %get-tuple-element.50) | copy-start | bytes 393220
  412.6 1.0 copy-start.2
  499.9 1.2 copy-start.4
  657.1 12.0 %copy-start.1 = (bf16[32,4096]{1,0:T(8,128)(2,1)S(1)}, bf16[32,4096]{1,0:T(8,128)(2,1)}, u32[]{:S(2)}) copy-start(bf16[32,4096]{1,0:T(8,128)(2,1)} %param.5) | copy-start | bytes 786436
Sparse Core Ops, SparseCore 0:
  26.2 86.4 all-gather.2
  249.2 74.5 all-gather.4
